TPU v7x, 256 devices: a whole 4x4x8 slice. The times are simulated.
256 devices in a mesh: req: 16 (over y, x), kv: 8 (over z), blk: 2 (over core).
Axes of the slice: x: 4, y: 4, z: 8, core: 2. Of those that a mesh axis runs over, the one named last changes fastest.
Arguments:
- x_resid: bfloat16 [16, 256, 5120], P('req', ('kv', 'blk')), may hold values from -54 to 54
- q_new: bfloat16 [16, 256, 4096], P('req', None, 'kv'), may hold values from -36 to 36
- k_new: bfloat16 [16, 256, 1024], P('req', None, 'kv'), may hold values from -6 to 12
- v_new: bfloat16 [16, 256, 1024], P('req', None, 'kv'), may hold values from -24 to 24
- k_cache: bfloat16 [16, 8, 64, 128, 128], P('req', 'kv', 'blk'), may hold values from -6 to 12
- v_cache: bfloat16 [16, 8, 64, 128, 128], P('req', 'kv', 'blk'), may hold values from -24 to 24
- cache_len: int32 [16], P('req'), may hold values from 1 to 7936, as said below
- page_table: int32 [16, 64], P('req'), may hold values from 0 to 63, as said below
- wo: bfloat16 [4096, 5120], P(('kv', 'blk')), may hold values from -0.09375 to 0.09375
- norm_gain: bfloat16 [5120], replicated, may hold values from 0.099609375 to 1.8984375
- w_gate: bfloat16 [5120, 7168], P('req', ('kv', 'blk')), may hold values from -0.078125 to 0.078125
- w_up: bfloat16 [5120, 7168], P('req', ('kv', 'blk')), may hold values from -0.078125 to 0.078125
- w_down: bfloat16 [7168, 5120], P(('kv', 'blk'), 'req'), may hold values from -0.0625 to 0.0625
Outputs:
- layer_out: bfloat16 [16, 256, 5120], P('req', ('kv', 'blk'))
- k_cache_out: bfloat16 [16, 8, 64, 128, 128], P('req', 'kv', 'blk')
- v_cache_out: bfloat16 [16, 8, 64, 128, 128], P('req', 'kv', 'blk')
Inputs may be any that keep to these rules, and one draw needn't show every extreme that they name: `cache_len`: at least one request has the largest length. `page_table`: each row is a permutation of 0 to 63.
All inputs are finite; a program needn't handle non-finite values.
Results may differ from a plain program's by a relative error of at most 0.0095.
Values may be sent and summed in bfloat16 or wider, within the bound.
A program may use at most 128 MiB of HBM per device.

v0:
```python
import math
import jax
import jax.numpy as jnp
from jax import lax
from jax.sharding import PartitionSpec as P


def combined_all(part, axis, combine):
    gathered = jax.tree.map(lambda a: lax.all_gather(a, axis), part)

    def take(source):
        return jax.tree.map(lambda a: lax.dynamic_index_in_dim(a, source, 0, False), gathered)

    return lax.fori_loop(
        1, lax.axis_size(axis), lambda source, state: combine(state, take(source)), take(0)
    )


def rotate(field, positions):
    half_width = field.shape[-1] // 2
    pair_index = jnp.arange(half_width, dtype=jnp.float32)
    frequency = jnp.power(1000000.0, -2.0 * pair_index / field.shape[-1])
    angles = positions.astype(jnp.float32)[:, None] * frequency[None, :]
    cosine = jnp.cos(angles)
    sine_part = jnp.sin(angles)
    lower_half = field[..., :half_width]
    upper_half = field[..., half_width:]
    return jnp.concatenate(
        [
            lower_half * cosine - upper_half * sine_part,
            upper_half * cosine + lower_half * sine_part,
        ],
        axis=-1,
    )


def merge_parts(first_part, second_part):
    max_first, total_first, out_first = first_part
    max_second, total_second, out_second = second_part
    overall = jnp.maximum(max_first, max_second)
    factor_first = jnp.exp(max_first - overall)
    factor_second = jnp.exp(max_second - overall)
    return (
        overall,
        factor_first * total_first + factor_second * total_second,
        factor_first[..., None] * out_first + factor_second[..., None] * out_second,
    )


def fetch_down(w_down):
    return lax.all_gather(w_down, "req", axis=1, tiled=True)


def rms_rows(rows, norm_gain):
    return (
        rows
        * lax.rsqrt(jnp.mean(rows * rows, axis=-1, keepdims=True) + 1e-05)
        * norm_gain.astype(jnp.float32)
    ).astype(jnp.bfloat16)


def on_device(
    x_resid,
    q_new,
    k_new,
    v_new,
    k_cache,
    v_cache,
    cache_len,
    page_table,
    wo,
    norm_gain,
    w_gate,
    w_up,
    w_down,
):
    blk_count = lax.axis_size("blk")
    blk_id = lax.axis_index("blk")
    new_tokens = q_new.shape[1]
    head_dim = k_new.shape[2]
    group_size = q_new.shape[2] // head_dim
    slot_count = k_cache.shape[2]
    page_size = k_cache.shape[3]
    page_total = page_table.shape[1]
    length = cache_len[0]
    positions = length + jnp.arange(new_tokens, dtype=jnp.int32)
    query_heads = rotate(
        q_new[0].reshape(new_tokens, group_size, head_dim).astype(jnp.float32).transpose(1, 0, 2),
        positions,
    ).astype(jnp.bfloat16)
    fresh_keys = rotate(k_new[0].astype(jnp.float32), positions).astype(jnp.bfloat16)
    page_ids = jnp.arange(page_total, dtype=jnp.int32)
    physical = blk_id * slot_count + jnp.arange(slot_count, dtype=jnp.int32)
    logical = jnp.sum(
        jnp.where(page_table[0][None, :] == physical[:, None], page_ids[None, :], 0), axis=1
    )
    slot_position = (
        logical[:, None] * page_size + jnp.arange(page_size, dtype=jnp.int32)[None, :]
    ).reshape(slot_count * page_size)
    new_index = slot_position - length
    is_new = (new_index >= 0) & (new_index < new_tokens)
    chosen = jnp.clip(new_index, 0, new_tokens - 1)
    key_rows = jnp.where(
        is_new[:, None], fresh_keys[chosen], k_cache[0, 0].reshape(slot_count * page_size, head_dim)
    )
    value_rows = jnp.where(
        is_new[:, None], v_new[0][chosen], v_cache[0, 0].reshape(slot_count * page_size, head_dim)
    )
    scores = jnp.einsum(
        "qd,sd->qs",
        query_heads.reshape(group_size * new_tokens, head_dim),
        key_rows,
        preferred_element_type=jnp.float32,
    ) * (1.0 / math.sqrt(head_dim))
    scores = scores.reshape(group_size, new_tokens, slot_count * page_size)
    allowed = slot_position[None, None, :] <= positions[None, :, None]
    masked = jnp.where(allowed, scores, -1e30)
    block_max = jnp.max(masked, axis=-1)
    weights = jnp.where(allowed, jnp.exp(masked - block_max[..., None]), 0.0).astype(jnp.bfloat16)
    block_total = jnp.sum(weights.astype(jnp.float32), axis=-1)
    block_out = jnp.einsum("gcs,sd->gcd", weights, value_rows, preferred_element_type=jnp.float32)
    merged = combined_all((block_max, block_total, block_out), "blk", merge_parts)
    attn = (merged[2] / merged[1][..., None]).astype(jnp.bfloat16)
    per_core = group_size // blk_count
    mine = lax.dynamic_slice_in_dim(attn, blk_id * per_core, per_core, 0)
    mine_rows = mine.transpose(1, 0, 2).reshape(new_tokens, per_core * head_dim)
    token_rows = x_resid.shape[1]
    row_start = lax.axis_index(("kv", "blk")) * token_rows
    partial_value = jnp.dot(mine_rows, wo, preferred_element_type=jnp.float32)
    own_part = lax.dynamic_slice_in_dim(partial_value, row_start, token_rows, 0) + x_resid[
        0
    ].astype(jnp.float32)
    contrib = lax.dynamic_update_slice_in_dim(partial_value, own_part, row_start, 0)
    resid = lax.psum(contrib, ("kv", "blk"))
    normed = rms_rows(resid, norm_gain)
    own_resid = lax.dynamic_slice_in_dim(resid, row_start, token_rows, 0)
    gate_val = jnp.dot(
        normed,
        lax.all_gather(w_gate, "req", axis=0, tiled=True),
        preferred_element_type=jnp.float32,
    )
    up_val = jnp.dot(
        normed, lax.all_gather(w_up, "req", axis=0, tiled=True), preferred_element_type=jnp.float32
    )
    hidden = (jax.nn.silu(gate_val) * up_val).astype(jnp.bfloat16)
    down_full = fetch_down(w_down)
    mlp_rows = lax.psum_scatter(
        jnp.dot(hidden, down_full, preferred_element_type=jnp.float32).astype(jnp.bfloat16),
        ("kv", "blk"),
        scatter_dimension=0,
        tiled=True,
    ).astype(jnp.float32)
    layer_out = (own_resid + mlp_rows).astype(jnp.bfloat16)[None]
    return (layer_out, key_rows.reshape(k_cache.shape), value_rows.reshape(v_cache.shape))


def solution(mesh):
    in_specs = (
        P("req", ("kv", "blk"), None),
        P("req", None, "kv"),
        P("req", None, "kv"),
        P("req", None, "kv"),
        P("req", "kv", "blk", None, None),
        P("req", "kv", "blk", None, None),
        P("req"),
        P("req", None),
        P(("kv", "blk"), None),
        P(),
        P("req", ("kv", "blk")),
        P("req", ("kv", "blk")),
        P(("kv", "blk"), "req"),
    )
    out_specs = (
        P("req", ("kv", "blk"), None),
        P("req", "kv", "blk", None, None),
        P("req", "kv", "blk", None, None),
    )
    return jax.shard_map(
        on_device, mesh=mesh, in_specs=in_specs, out_specs=out_specs, check_vma=False
    )
```

profile of v0, /device:TPU:2, one launch (start us, length us, event | category | flops | bytes accessed | tf_op | source)
XLA Modules:
  0.0 365.1 jit_solution(288112992523952814)
XLA Ops:
  11.4 1.9 reshape.295
  13.3 1.3 copy.30
  14.8 15.0 %gather_fusion = bf16[4096,128]{1,0:T(8,128)(2,1)} fusion(bf16[256,128]{1,0:T(8,128)(2,1)S(1)} %copy.32, s32[4096]{0:T(1024)S(1)} %broadcast_clamp_fusion), kind=kCustom, calls=%fused_computation | custom fusion | bytes 2113536 | tf_op jit(solution)/shard_map/gather | solution.py:104
  29.8 15.0 %gather_fusion.1 = bf16[4096,128]{1,0:T(8,128)(2,1)} fusion(bf16[256,128]{1,0:T(8,128)(2,1)S(1)} %bitcast.87, s32[4096]{0:T(1024)S(1)} %broadcast_clamp_fusion), kind=kCustom, calls=%fused_computation.1 | custom fusion | bytes 2113536 | tf_op jit(solution)/shard_map/gather | solution.py:107
  45.6 3.6 bitcast_select_fusion.2
  49.2 3.7 %fusion.1 = (f32[1024]{0:T(1024)S(1)}, f32[1024,4096]{1,0:T(8,128)S(1)}) fusion(pred[256,4096]{1,0:T(8,128)(4,1)S(1)} %broadcast_compare_fusion, bf16[4096,128]{1,0:T(8,128)(2,1)S(1)} %bitcast_select_fusion.2, bf16[1024,64]{0,1:T(8,128)(2,1)S(1)} %bitcast.95, bf16[1024,64]{0,1:T(8,128)(2,1)S(1)} %bitcast.94), kind=kOutput, calls=%fused_computation.6 | convolution fusion | flops 1086848000 | bytes 19140608 | tf_op jit(solution)/shard_map/qd,sd->qs/dot_general | solution.py:109
  52.9 6.7 %convert_reduce_fusion = (f32[1024]{0:T(1024)S(1)}, bf16[1024,4096]{1,0:T(8,128)(2,1)S(1)}) fusion(f32[1024]{0:T(1024)S(1)} %get-tuple-element.46, f32[1024,4096]{1,0:T(8,128)S(1)} %get-tuple-element.47, pred[256,4096]{1,0:T(8,128)(4,1)S(1)} %broadcast_compare_fusion), kind=kLoop, calls=%fused_computation.5 | loop fusion | flops 29359104 | bytes 26222592 | tf_op jit(solution)/shard_map/reduce_sum | solution.py:120
  59.7 1.5 broadcast_select_fusion
  61.2 1.0 copy-done.6
  62.2 3.2 fusion.34
  65.4 1.8 all_gather.32
  67.3 2.0 all_gather.28
  69.3 13.5 %all-gather.12.cloned.1.call-done = f32[8,256,128]{2,1,0:T(8,128)} async-done(((f32[4,256,128]{2,1,0:T(8,128)}), f32[8,256,128]{2,1,0:T(8,128)}) %all-gather.12.cloned.1.call-update) | async-done | bytes 1048592 | tf_op jit(solution)/shard_map/all_gather | solution.py:9
  82.8 1.3 fusion.33
  85.1 1.0 divide_convert_fusion
  86.2 3.2 fusion.35
  89.4 1.7 fusion.8
  92.9 126.8 %all-reduce.2.cloned.1.call-done = f32[256,5120]{1,0:T(8,128)} async-done(((f32[256,5120]{1,0:T(8,128)}), f32[256,5120]{1,0:T(8,128)}) %all-reduce.2.cloned.1.call-update) | async-done | bytes 5242896 | tf_op jit(solution)/shard_map/psum | solution.py:134
  219.8 2.9 multiply_reduce_fusion
  222.7 6.2 %fusion.29 = f32[256,448]{0,1:T(8,128)S(1)} fusion(bf16[5120,448]{1,0:T(8,128)(2,1)} %all-gather.6.cloned.1.call-done, f32[256,5120]{1,0:T(8,128)} %all-reduce.2.cloned.1.call-done, f32[5120]{0:T(1024)S(1)} %convert_element_type.69, f32[256]{0:T(256)S(1)} %add_rsqrt_fusion), kind=kOutput, calls=%fused_computation.74 | convolution fusion | flops 1178337280 | bytes 10310656 | tf_op jit(solution)/shard_map/dot_general | solution.py:137
  228.9 53.8 %all-gather.8.cloned.1.call-done = bf16[5120,448]{1,0:T(8,128)(2,1)} async-done(((bf16[320,448]{1,0:T(8,128)(2,1)}), bf16[5120,448]{1,0:T(8,128)(2,1)}) %all-gather.8.cloned.1.call-update) | async-done | bytes 4587536 | tf_op jit(solution)/shard_map/all_gather | solution.py:143
  282.8 12.4 %convolution_convert_fusion = bf16[256,5120]{1,0:T(8,128)(2,1)} fusion(bf16[448,5120]{0,1:T(8,128)(2,1)} %all-gather.10.cloned.1.call-done, bf16[5120,448]{1,0:T(8,128)(2,1)} %all-gather.8.cloned.1.call-done, f32[256,448]{0,1:T(8,128)S(1)} %fusion.29, f32[256,5120]{1,0:T(8,128)} %all-reduce.2.cloned.1.call-done, f32[5120]{0:T(1024)S(1)} %convert_element_type.69, ...), kind=kOutput, calls=%fused_computation.7 | convolution fusion | flops 2354741248 | bytes 17519616 | tf_op jit(solution)/shard_map/dot_general | solution.py:148
  295.2 60.8 %reduce-scatter.2.cloned.1.call-done = bf16[16,5120]{1,0:T(8,128)(2,1)} async-done(((bf16[256,5120]{1,0:T(8,128)(2,1)}), bf16[16,5120]{1,0:T(8,128)(2,1)}) %reduce-scatter.2.cloned.1.call-update) | async-done | bytes 163856 | tf_op jit(solution)/shard_map/reduce_scatter | solution.py:147
  356.0 1.8 fusion.14
  (62 shorter events, 6.4 us)
Async XLA Ops:
  8.0 78.2 %copy-start = (bf16[256,5120]{1,0:T(8,128)(2,1)S(1)}, bf16[256,5120]{1,0:T(8,128)(2,1)}, u32[]{:S(2)}) copy-start(bf16[256,5120]{1,0:T(8,128)(2,1)} %param.21) | copy-start | bytes 7864324
  8.0 74.8 %all-gather.12.cloned.1.call-start = ((), (), s32[]{:S(2)}) async-start(), calls=%async_computation.6 | async-start | bytes 1572864 | tf_op jit(solution)/shard_map/all_gather | solution.py:9
  14.6 15.2 %copy-start.1 = (bf16[1,256,128]{2,1,0:T(8,128)(2,1)S(1)}, bf16[1,256,128]{2,1,0:T(8,128)(2,1)}, u32[]{:S(2)}) copy-start(bf16[1,256,128]{2,1,0:T(8,128)(2,1)} %param.16) | copy-start | bytes 196612
  52.9 6.8 %copy-start.2 = (bf16[4096,128]{1,0:T(8,128)(2,1)S(1)}, bf16[4096,128]{1,0:T(8,128)(2,1)}, u32[]{:S(2)}) copy-start(bf16[4096,128]{1,0:T(8,128)(2,1)} %gather_fusion) | copy-start | bytes 3145732
  52.9 6.8 %copy-start.3 = (bf16[4096,128]{1,0:T(8,128)(2,1)S(1)}, bf16[4096,128]{1,0:T(8,128)(2,1)}, u32[]{:S(2)}) copy-start(bf16[4096,128]{1,0:T(8,128)(2,1)} %gather_fusion.1) | copy-start | bytes 3145732
  52.9 6.8 %copy-start.4 = (bf16[1,1,32,128,128]{4,3,2,1,0:T(8,128)(2,1)S(1)}, bf16[1,1,32,128,128]{4,3,2,1,0:T(8,128)(2,1)}, u32[]{:S(2)}) copy-start(bf16[1,1,32,128,128]{4,3,2,1,0:T(8,128)(2,1)} %param.17) | copy-start | bytes 3145732
  52.9 6.8 %copy-start.5 = (bf16[1,1,32,128,128]{4,3,2,1,0:T(8,128)(2,1)S(1)}, bf16[1,1,32,128,128]{4,3,2,1,0:T(8,128)(2,1)}, u32[]{:S(2)}) copy-start(bf16[1,1,32,128,128]{4,3,2,1,0:T(8,128)(2,1)} %param.18) | copy-start | bytes 3145732
  61.2 1.0 copy-start.6
  65.4 154.4 %all-reduce.2.cloned.1.call-start = ((), (), s32[]{:S(2)}) async-start(), calls=%async_computation.1 | async-start | bytes 10485760 | tf_op jit(solution)/shard_map/psum | solution.py:134
  85.0 4.4 %copy-start.7 = (bf16[1,16,5120]{2,1,0:T(8,128)(2,1)S(1)}, bf16[1,16,5120]{2,1,0:T(8,128)(2,1)}, u32[]{:S(2)}) copy-start(bf16[1,16,5120]{2,1,0:T(8,128)(2,1)} %param.13) | copy-start | bytes 491524
  89.4 3.6 copy-start.8
  91.1 131.6 %all-gather.6.cloned.1.call-start = ((), (), s32[]{:S(2)}) async-start(), calls=%async_computation.2 | async-start | bytes 5570560 | tf_op jit(solution)/shard_map/all_gather | solution.py:139
  91.7 137.2 %all-gather.10.cloned.1.call-start = ((), (), s32[]{:S(2)}) async-start(), calls=%async_computation.4 | async-start | bytes 5570560 | tf_op jit(solution)/shard_map/all_gather | solution.py:51
  92.3 190.5 %all-gather.8.cloned.1.call-start = ((), (), s32[]{:S(2)}) async-start(), calls=%async_computation.3 | async-start | bytes 5570560 | tf_op jit(solution)/shard_map/all_gather | solution.py:143
  92.9 263.1 %reduce-scatter.2.cloned.1.call-start = ((), (), s32[]{:S(2)}) async-start(), calls=%async_computation.5 | async-start | bytes 2785280 | tf_op jit(solution)/shard_map/reduce_scatter | solution.py:147
Sparse Core Ops, SparseCore 0:
  65.5 17.2 all-gather.11
  91.2 128.4 all-reduce.1
  295.3 60.6 reduce-scatter.1
Sparse Core Ops, SparseCore 1:
  94.0 62.4 all-gather.5
  158.8 60.7 all-gather.9
  221.9 60.8 all-gather.7
where the time goes:
time: 365 us
  waiting for transfers between devices  257 us (70%)
  local copies, waits for them, and re-layouts  37.7 us (10%)
  matrix products  28.6 us (8%)
  other arithmetic  21.5 us (6%)
  between operations  16.6 us (5%)
  blocking collectives  3.81 us (1%)
    psum x1, waiting for transfers between devices, on_device(): resid = lax.psum(contrib, ('kv', 'blk'))  127 us
    reduce_scatter x1, waiting for transfers between devices, on_device(): lax.psum_scatter(jnp.dot(hidden, down_full, preferred_element_type=jnp.fl...  60.8 us
    all_gather x1, waiting for transfers between devices, on_device(): lax.all_gather(w_up, 'req', axis=0, tiled=True)  53.8 us
    gather x1, local copies, waits for them, and re-layouts, on_device(): fresh_keys[chosen]  15 us
    gather x1, local copies, waits for them, and re-layouts, on_device(): v_new[0][chosen]  15 us
    all_gather x1, waiting for transfers between devices, combined_all(): gathered = jax.tree.map(lambda a: lax.all_gather(a, axis), part)  13.5 us
    dot_general x1, matrix products, on_device(): jnp.dot(hidden, down_full, preferred_element_type=jnp.float32)  12.4 us
  transfers between devices with their start and end apart: 6, of which 4 were waited for; matrix products, arithmetic and copies ran while one was open for 2% of the time, Pallas kernels for 0%

commit v1 on v0

--- a/solution.py
+++ b/solution.py
@@ -1,8 +1,16 @@
+import functools
 import math
 import jax
 import jax.numpy as jnp
 from jax import lax
 from jax.sharding import PartitionSpec as P
+
+
+def scenes_push(a0, a_name):
+    return lax.all_gather(a0, axis_name=a_name).sum(axis=0)
+
+
+guide_shapes = functools.partial(scenes_push, a_name=("kv", "blk"))
 
 
 def combined_all(part, axis, combine):
@@ -131,7 +139,7 @@
         0
     ].astype(jnp.float32)
     contrib = lax.dynamic_update_slice_in_dim(partial_value, own_part, row_start, 0)
-    resid = lax.psum(contrib, ("kv", "blk"))
+    resid = guide_shapes(contrib)
     normed = rms_rows(resid, norm_gain)
     own_resid = lax.dynamic_slice_in_dim(resid, row_start, token_rows, 0)
     gate_val = jnp.dot(

time: 365 us -> 773 us (2.12)
  waiting for transfers between devices: 257 us -> 638 us
  other arithmetic: 21.5 us -> 49.4 us
    all_gather x0 -> x1, waiting for transfers between devices: none -> 411 us  [scenes_push(): return lax.all_gather(a0, axis_name=a_name).sum(axis=0)]
    psum x1 -> x0, waiting for transfers between devices: 127 us -> none  [on_device(): resid = lax.psum(contrib, ('kv', 'blk'))]
    all_gather x1, waiting for transfers between devices: 0.03 us -> 63.3 us  [fetch_down(): return lax.all_gather(w_down, 'req', axis=1, tiled=True)]
    all_gather x1, waiting for transfers between devices: 0.03 us -> 30.4 us  [on_device(): lax.all_gather(w_gate, 'req', axis=0, tiled=True)]
    reduce_sum x0 -> x1, other arithmetic: none -> 28.9 us  [scenes_push(): return lax.all_gather(a0, axis_name=a_name).sum(axis=0)]
  transfers between devices with their start and end apart: 6 -> 6, of which waited for: 4 -> 6; matrix products, arithmetic and copies ran while one was open for 2% -> 5% of each run, Pallas kernels for 0% -> 0%
where the time goes in v1:
time: 773 us
  waiting for transfers between devices  638 us (83%)
  other arithmetic  49.4 us (6%)
  local copies, waits for them, and re-layouts  40 us (5%)
  matrix products  26.4 us (3%)
  between operations  15.2 us (2%)
    all_gather x1, waiting for transfers between devices, scenes_push(): return lax.all_gather(a0, axis_name=a_name).sum(axis=0)  411 us
    all_gather x1, waiting for transfers between devices, fetch_down(): return lax.all_gather(w_down, 'req', axis=1, tiled=True)  63.3 us
    reduce_scatter x1, waiting for transfers between devices, on_device(): lax.psum_scatter(jnp.dot(hidden, down_full, preferred_element_type=jnp.fl...  60.7 us
    all_gather x1, waiting for transfers between devices, on_device(): lax.all_gather(w_up, 'req', axis=0, tiled=True)  57.1 us
    all_gather x1, waiting for transfers between devices, on_device(): lax.all_gather(w_gate, 'req', axis=0, tiled=True)  30.4 us
    reduce_sum x1, other arithmetic, scenes_push(): return lax.all_gather(a0, axis_name=a_name).sum(axis=0)  28.9 us
  transfers between devices with their start and end apart: 6, of which 6 were waited for; matrix products, arithmetic and copies ran while one was open for 5% of the time, Pallas kernels for 0%

profile of v1, /device:TPU:2, one launch (start us, length us, event | category | flops | bytes accessed | tf_op | source)
XLA Modules:
  0.0 772.8 jit_solution(13690909916491767472)
XLA Ops:
  10.5 1.9 reshape.297
  12.4 1.3 copy.30
  13.9 15.0 %gather_fusion = bf16[4096,128]{1,0:T(8,128)(2,1)} fusion(bf16[256,128]{1,0:T(8,128)(2,1)S(1)} %copy.32, s32[4096]{0:T(1024)S(1)} %broadcast_clamp_fusion), kind=kCustom, calls=%fused_computation | custom fusion | bytes 2113536 | tf_op jit(solution)/shard_map/gather | solution.py:112
  29.0 15.0 %gather_fusion.1 = bf16[4096,128]{1,0:T(8,128)(2,1)} fusion(bf16[256,128]{1,0:T(8,128)(2,1)S(1)} %bitcast.92, s32[4096]{0:T(1024)S(1)} %broadcast_clamp_fusion), kind=kCustom, calls=%fused_computation.1 | custom fusion | bytes 2113536 | tf_op jit(solution)/shard_map/gather | solution.py:115
  44.7 3.6 bitcast_select_fusion.2
  48.3 3.7 fusion.1
  52.1 6.7 convert_reduce_fusion
  58.9 1.5 broadcast_select_fusion
  61.3 3.2 fusion.35
  64.6 1.8 all_gather.40
  66.4 2.0 all_gather.36
  68.5 13.5 %all-gather.15.cloned.1.call-done = f32[8,256,128]{2,1,0:T(8,128)} async-done(((f32[4,256,128]{2,1,0:T(8,128)}), f32[8,256,128]{2,1,0:T(8,128)}) %all-gather.15.cloned.1.call-update) | async-done | bytes 1048592 | tf_op jit(solution)/shard_map/all_gather | solution.py:17
  82.0 1.3 fusion.34
  86.2 2.3 copy.41
  91.3 410.9 %all-gather.7.cloned.1.call-done = f32[16,256,5120]{2,1,0:T(8,128)} async-done(((f32[1,256,5120]{2,1,0:T(8,128)}), f32[16,256,5120]{2,1,0:T(8,128)}) %all-gather.7.cloned.1.call-update) | async-done | bytes 83886096 | tf_op jit(solution)/shard_map/all_gather | solution.py:10
  502.2 28.9 %reduce_sum.38 = f32[256,5120]{1,0:T(8,128)} reduce(f32[16,256,5120]{2,1,0:T(8,128)} %all-gather.7.cloned.1.call-done, f32[]{:T(128)} %constant.66.clone.1), dimensions={0}, to_apply=%region_3.4 | reduce | flops 19660800 | bytes 89128960 | tf_op jit(solution)/shard_map/reduce_sum | solution.py:10
  531.1 2.9 multiply_reduce_fusion
  534.0 30.4 %all-gather.9.cloned.1.call-done = bf16[5120,448]{1,0:T(8,128)(2,1)} async-done(((bf16[320,448]{1,0:T(8,128)(2,1)}), bf16[5120,448]{1,0:T(8,128)(2,1)}) %all-gather.9.cloned.1.call-update) | async-done | bytes 4587536 | tf_op jit(solution)/shard_map/all_gather | solution.py:147
  564.4 6.1 fusion.30
  570.6 57.1 %all-gather.11.cloned.1.call-done = bf16[5120,448]{1,0:T(8,128)(2,1)} async-done(((bf16[320,448]{1,0:T(8,128)(2,1)}), bf16[5120,448]{1,0:T(8,128)(2,1)}) %all-gather.11.cloned.1.call-update) | async-done | bytes 4587536 | tf_op jit(solution)/shard_map/all_gather | solution.py:151
  627.7 63.3 %all-gather.13.cloned.1.call-done = bf16[448,5120]{0,1:T(8,128)(2,1)} async-done(((bf16[448,320]{0,1:T(8,128)(2,1)}), bf16[448,5120]{0,1:T(8,128)(2,1)}) %all-gather.13.cloned.1.call-update) | async-done | bytes 4587536 | tf_op jit(solution)/shard_map/all_gather | solution.py:59
  691.0 12.5 %convolution_convert_fusion = bf16[256,5120]{1,0:T(8,128)(2,1)} fusion(bf16[448,5120]{0,1:T(8,128)(2,1)} %all-gather.13.cloned.1.call-done, bf16[5120,448]{1,0:T(8,128)(2,1)} %all-gather.11.cloned.1.call-done, f32[256,448]{0,1:T(8,128)S(1)} %fusion.30, f32[256,5120]{1,0:T(8,128)} %reduce_sum.38, f32[5120]{0:T(1024)S(1)} %convert_element_type.69, ...), kind=kOutput, calls=%fused_computation.7 | convolution fusion | flops 2354741248 | bytes 17519616 | tf_op jit(solution)/shard_map/dot_general | solution.py:156
  703.5 60.7 %reduce-scatter.2.cloned.1.call-done = bf16[16,5120]{1,0:T(8,128)(2,1)} async-done(((bf16[256,5120]{1,0:T(8,128)(2,1)}), bf16[16,5120]{1,0:T(8,128)(2,1)}) %reduce-scatter.2.cloned.1.call-update) | async-done | bytes 163856 | tf_op jit(solution)/shard_map/reduce_scatter | solution.py:155
  764.2 1.8 fusion.15
  (66 shorter events, 10.1 us)
Async XLA Ops:
  7.2 78.1 %copy-start = (bf16[256,5120]{1,0:T(8,128)(2,1)S(1)}, bf16[256,5120]{1,0:T(8,128)(2,1)}, u32[]{:S(2)}) copy-start(bf16[256,5120]{1,0:T(8,128)(2,1)} %param.21) | copy-start | bytes 7864324
  7.2 74.8 %all-gather.15.cloned.1.call-start = ((), (), s32[]{:S(2)}) async-start(), calls=%async_computation.6 | async-start | bytes 1572864 | tf_op jit(solution)/shard_map/all_gather | solution.py:17
  13.7 15.2 %copy-start.2 = (bf16[1,256,128]{2,1,0:T(8,128)(2,1)S(1)}, bf16[1,256,128]{2,1,0:T(8,128)(2,1)}, u32[]{:S(2)}) copy-start(bf16[1,256,128]{2,1,0:T(8,128)(2,1)} %param.16) | copy-start | bytes 196612
  52.1 6.8 copy-start.3
  52.1 6.8 copy-start.4
  52.1 6.8 copy-start.5
  52.1 6.8 copy-start.6
  60.4 1.0 copy-start.7
  64.5 437.7 %all-gather.7.cloned.1.call-start = ((), (), s32[]{:S(2)}) async-start(), calls=%async_computation.1 | async-start | bytes 89128960 | tf_op jit(solution)/shard_map/all_gather | solution.py:10
  86.2 2.4 copy-start.8
  88.5 2.7 copy-start.9
  89.3 475.1 %all-gather.9.cloned.1.call-start = ((), (), s32[]{:S(2)}) async-start(), calls=%async_computation.2 | async-start | bytes 5570560 | tf_op jit(solution)/shard_map/all_gather | solution.py:147
  90.1 537.7 %all-gather.11.cloned.1.call-start = ((), (), s32[]{:S(2)}) async-start(), calls=%async_computation.3 | async-start | bytes 5570560 | tf_op jit(solution)/shard_map/all_gather | solution.py:151
  90.6 600.4 %all-gather.13.cloned.1.call-start = ((), (), s32[]{:S(2)}) async-start(), calls=%async_computation.4 | async-start | bytes 5570560 | tf_op jit(solution)/shard_map/all_gather | solution.py:59
  91.2 673.0 %reduce-scatter.2.cloned.1.call-start = ((), (), s32[]{:S(2)}) async-start(), calls=%async_computation.5 | async-start | bytes 2785280 | tf_op jit(solution)/shard_map/reduce_scatter | solution.py:155
  691.0 74.9 %copy-start.1 = (bf16[256,5120]{1,0:T(8,128)(2,1)S(1)}, bf16[256,5120]{1,0:T(8,128)(2,1)}, u32[]{:S(2)}) copy-start(bf16[256,5120]{1,0:T(8,128)(2,1)} %param.21) | copy-start | bytes 7864324
Sparse Core Ops, SparseCore 0:
  64.6 17.3 all-gather.14
  89.4 412.7 all-gather.6
  504.6 59.7 all-gather.8
  566.7 60.9 all-gather.10
  630.0 60.9 all-gather.12
  703.7 60.4 reduce-scatter.1
